TPU v7x, 32 devices: a whole 2x2x4 slice. The times are simulated.
32 devices in a mesh: wide: 8 (over y, x, core), narrow: 4 (over z).
Axes of the slice: x: 2, y: 2, z: 4, core: 2. Of those that a mesh axis runs over, the one named last changes fastest.
Arguments:
- hidden: bfloat16 [8, 256, 2048], P('wide', None, 'narrow'), may hold values from -6 to 6
- norm_gain: bfloat16 [2, 2048], replicated, may hold values from 0.25 to 1.75
- w_qkv: bfloat16 [2048, 3, 2048], P(None, None, 'narrow'), may hold values from -1 to 1
- qk_gain: float32 [2, 2048], P(None, 'narrow'), may hold values from 0.25 to 32
- w_out: bfloat16 [2048, 2048], P('narrow'), may hold values from -0.125 to 0.125
- cache: bfloat16 [2, 8, 2048, 2048], P(None, 'wide', None, 'narrow'), may hold values from -6 to 6
- lengths: int32 [8], replicated, may hold values from 1 to 2048, 8192 in all
- placing: int32 [8], replicated, may hold values from 0 to 7, each once
- routes: int32 [8, 256, 8], P('wide'), may hold values from 0 to 15, all different within a row; in each aligned block of 256 rows (0 to 255, 256 to 511, ..., all dimensions but the last counted through in order) at most 192 rows name the same one
- gate_w: float32 [8, 256, 8], P('wide'), may hold values from 0.02 to 0.3
- w_gu: bfloat16 [16, 2048, 2, 1024], P('wide', None, None, 'narrow'), may hold values from -0.125 to 0.125
- w_down: bfloat16 [16, 1024, 2048], P('wide', 'narrow'), may hold values from -0.1875 to 0.1875
Outputs:
- result: bfloat16 [8, 256, 2048], P('wide', None, 'narrow')
- new_cache: bfloat16 [2, 8, 256, 2048], P(None, 'wide', None, 'narrow')
Inputs may be any that keep to these rules, and one draw needn't show every extreme that they name: `routes`: each token names 8 different experts; among the 256 tokens of one request no expert is named more than 192 times. `lengths`: some request has 2048 cached positions. Slot s holds request placing[s]; every request is held once.
All inputs are finite; a program needn't handle non-finite values.
Results may differ from a plain program's by a relative error of at most 0.013.
Values may be sent and summed in bfloat16 or wider, within the bound.
A program may use at most 128 MiB of HBM per device.

v0:
```python
import jax
import jax.numpy as jnp
from jax import lax
from jax.sharding import PartitionSpec as P

HD = 128


def normalize(values, gain_row):
    values = values.astype(jnp.float32)
    return (
        values
        * lax.rsqrt(jnp.mean(values * values, axis=-1, keepdims=True) + 1e-05)
        * gain_row.astype(jnp.float32)
    )


def rotary(values, positions):
    half_dim = values.shape[-1] // 2
    frequency = 10000.0 ** (-(jnp.arange(half_dim, dtype=jnp.float32) * (2.0 / values.shape[-1])))
    angle = positions[:, None] * frequency[None, :]
    cosine = jnp.cos(angle)[:, None, :]
    sine_part = jnp.sin(angle)[:, None, :]
    first_half = values[..., :half_dim]
    second_half = values[..., half_dim:]
    return jnp.concatenate(
        [
            first_half * cosine - second_half * sine_part,
            second_half * cosine + first_half * sine_part,
        ],
        axis=-1,
    )


def per_device(
    hidden, norm_gain, w_qkv, qk_gain, w_out, cache, lengths, placing, routes, gate_w, w_gu, w_down
):
    narrow = lax.axis_size("narrow")
    wide_size = lax.axis_size("wide")
    column = lax.axis_index("narrow")
    position = lax.axis_index("wide")
    span_len = hidden.shape[1]
    share_cols = hidden.shape[2]
    full_width = share_cols * narrow
    tokens = lax.all_gather(hidden[0], "narrow", axis=1, tiled=True)
    normed = normalize(tokens, norm_gain[0]).astype(jnp.bfloat16)
    local_cols = w_qkv.shape[2]
    projected = jnp.dot(
        normed, w_qkv.reshape(full_width, 3 * local_cols), preferred_element_type=jnp.float32
    )
    queries = projected[:, :local_cols]
    keys_new = projected[:, local_cols : 2 * local_cols]
    values_new = projected[:, 2 * local_cols :]
    squares = lax.psum((jnp.sum(queries * queries, -1), jnp.sum(keys_new * keys_new, -1)), "narrow")
    features = local_cols * narrow
    queries = queries * lax.rsqrt(squares[0][:, None] / features + 1e-05) * qk_gain[0]
    keys_new = keys_new * lax.rsqrt(squares[1][:, None] / features + 1e-05) * qk_gain[1]
    head_count = local_cols // HD
    length = lengths[placing[position]]
    positions = length.astype(jnp.float32) + jnp.arange(span_len, dtype=jnp.float32)
    queries = rotary(queries.reshape(span_len, head_count, HD), positions).astype(jnp.bfloat16)
    keys_new = rotary(keys_new.reshape(span_len, head_count, HD), positions).astype(jnp.bfloat16)
    values_new = values_new.reshape(span_len, head_count, HD).astype(jnp.bfloat16)
    stored = cache.shape[2]
    all_keys = jnp.concatenate([cache[0, 0].reshape(stored, head_count, HD), keys_new], 0)
    all_values = jnp.concatenate([cache[1, 0].reshape(stored, head_count, HD), values_new], 0)
    scores = jnp.einsum(
        "thd,jhd->htj", queries, all_keys, preferred_element_type=jnp.float32
    ) * HD ** (-0.5)
    key_index = jnp.arange(stored + span_len, dtype=jnp.int32)[None, :]
    query_index = jnp.arange(span_len, dtype=jnp.int32)[:, None]
    allowed = jnp.where(key_index < stored, key_index < length, key_index - stored <= query_index)
    scores = jnp.where(allowed[None], scores, -1e30)
    highest = jnp.max(scores, axis=-1, keepdims=True)
    exponent = jnp.exp(scores - highest)
    weights = exponent.astype(jnp.bfloat16)
    denominator = jnp.sum(exponent, axis=-1)
    summed = jnp.einsum("htj,jhd->thd", weights, all_values, preferred_element_type=jnp.float32)
    heads_out = (
        (summed / jnp.transpose(denominator)[:, :, None])
        .astype(jnp.bfloat16)
        .reshape(span_len, local_cols)
    )
    partial_out = jnp.dot(heads_out, w_out, preferred_element_type=jnp.float32)
    attention = lax.psum(partial_out.astype(jnp.bfloat16), "narrow").astype(jnp.float32)
    after = (tokens.astype(jnp.float32) + attention).astype(jnp.bfloat16)
    after_own = lax.dynamic_slice_in_dim(after, column * share_cols, share_cols, 1)
    routed = normalize(after, norm_gain[1]).astype(jnp.bfloat16)
    chosen = routes.shape[2]
    held_experts = w_gu.shape[0]
    experts = held_experts * wide_size
    capacity = span_len * chosen * 3 // (2 * experts)
    flat_routes = routes[0].reshape(-1)
    onehot = (flat_routes[:, None] == jnp.arange(experts, dtype=jnp.int32)[None, :]).astype(
        jnp.int32
    )
    slot_rank = jnp.sum((jnp.cumsum(onehot, 0) - onehot) * onehot, 1)
    target = flat_routes * capacity + slot_rank
    token_row = jnp.arange(span_len * chosen, dtype=jnp.int32) // chosen
    source_row = jnp.full((experts * capacity,), span_len, jnp.int32).at[target].set(token_row)
    padded = jnp.concatenate([routed, jnp.zeros((1, full_width), jnp.bfloat16)], 0)
    outgoing = padded[source_row].reshape(experts, capacity, full_width)
    arrived = lax.all_to_all(outgoing, "wide", split_axis=0, concat_axis=0, tiled=True)
    inner_cols = w_gu.shape[3]
    arrived = arrived.reshape(wide_size, held_experts, capacity, full_width)
    gate_up = jnp.einsum(
        "wjcd,jdf->wjcf",
        arrived,
        w_gu.reshape(held_experts, full_width, 2 * inner_cols),
        preferred_element_type=jnp.float32,
    )
    activated = (jax.nn.silu(gate_up[..., :inner_cols]) * gate_up[..., inner_cols:]).astype(
        jnp.bfloat16
    )
    parts = jnp.einsum(
        "wjcf,jfd->wjcd", activated, w_down, preferred_element_type=jnp.float32
    ).astype(jnp.bfloat16)
    gate_scale = gate_w[0].reshape(-1)
    returned = lax.all_to_all(
        parts.reshape(experts, capacity, full_width),
        "wide",
        split_axis=0,
        concat_axis=0,
        tiled=True,
    )
    picked = returned.reshape(experts * capacity, full_width)[target].astype(jnp.float32)
    combined = jnp.sum((picked * gate_scale[:, None]).reshape(span_len, chosen, full_width), 1)
    expert_out = lax.psum_scatter(
        combined.astype(jnp.bfloat16), "narrow", scatter_dimension=1, tiled=True
    ).astype(jnp.float32)
    result = (after_own.astype(jnp.float32) + expert_out).astype(jnp.bfloat16)[None]
    fresh = jnp.stack(
        [keys_new.reshape(span_len, local_cols), values_new.reshape(span_len, local_cols)]
    )[:, None]
    return (result, fresh)


def solution(mesh):
    placed = (
        P("wide", None, "narrow"),
        P(),
        P(None, None, "narrow"),
        P(None, "narrow"),
        P("narrow", None),
        P(None, "wide", None, "narrow"),
        P(),
        P(),
        P("wide", None, None),
        P("wide", None, None),
        P("wide", None, None, "narrow"),
        P("wide", "narrow", None),
    )
    return jax.shard_map(
        per_device,
        mesh=mesh,
        in_specs=placed,
        out_specs=(P("wide", None, "narrow"), P(None, "wide", None, "narrow")),
        check_vma=False,
    )
```

profile of v0, /device:TPU:0, one launch (start us, length us, event | category | flops | bytes accessed | tf_op | source)
XLA Modules:
  0.0 548.3 jit_solution(7301213833029315441)
XLA Ops:
  15.3 8.9 %copy.24 = bf16[2048,3,512]{0,2,1:T(8,128)(2,1)} copy(bf16[2048,3,512]{2,0,1:T(8,128)(2,1)} %param.14) | data formatting | bytes 12582912 | tf_op args[2]
  24.2 4.5 fusion.74
  28.7 4.0 copy.45
  32.7 4.0 copy.31
  36.7 4.0 copy.23
  40.8 4.5 reduce-window.6
  48.3 5.0 fusion.39
  55.2 13.6 %all-reduce.1 = (f32[256]{0:T(256)S(1)}, f32[256]{0:T(256)S(1)}) all-reduce(f32[256]{0:T(256)S(1)} %get-tuple-element.7, f32[256]{0:T(256)S(1)} %get-tuple-element.6), channel_id=1, replica_groups=mesh['wide'=8,'narrow'=4] {'narrow'}, use_global_device_ids=true, to_apply=%region_4.0 | all-reduce | flops 512 | bytes 4096 | tf_op jit(solution)/shard_map/psum | solution.py:54
  82.6 2.5 fusion.4
  85.1 2.6 fusion.49
  90.3 8.1 %scatter_custom_fusion = s32[3072]{0:T(1024)S(1)} fusion(s32[2048]{0:T(1024)S(1)} %bitcast.90, s32[2048]{0:T(1024)S(1)} %add_select_fusion, s32[]{:T(128)} %constant.66.clone.1), kind=kCustom, calls=%fused_computation.92 | custom fusion | bytes 12292 | tf_op jit(solution)/shard_map/scatter | solution.py:100
  98.4 41.4 %all-reduce.4.cloned.1.call-done = bf16[256,2048]{1,0:T(8,128)(2,1)} async-done(((bf16[256,2048]{1,0:T(8,128)(2,1)}), bf16[256,2048]{1,0:T(8,128)(2,1)}) %all-reduce.4.cloned.1.call-update) | async-done | bytes 1048592 | tf_op jit(solution)/shard_map/psum | solution.py:85
  142.9 16.0 %gather_fusion = bf16[3072,2048]{1,0:T(8,128)(2,1)} fusion(bf16[257,2048]{1,0:T(8,128)(2,1)S(1)} %concatenate.20, s32[3072]{0:T(1024)S(1)} %fusion.62), kind=kCustom, calls=%fused_computation | custom fusion | bytes 25178112 | tf_op jit(solution)/shard_map/gather | solution.py:102
  158.9 5.6 %all-to-all-start = ((bf16[16,192,2048]{2,1,0:T(8,128)(2,1)}), bf16[16,192,2048]{2,1,0:T(8,128)(2,1)}, u32[]{:S(2)}, u32[]{:S(2)}) async-start(bf16[16,192,2048]{2,1,0:T(8,128)(2,1)} %bitcast.81), calls=%async_computation | async-start | bytes 25165824 | tf_op jit(solution)/shard_map/all_to_all | solution.py:103
  164.5 7.7 %reshape.288 = bf16[2,2048,512,1]{2,1,0,3:T(8,128)(2,1)} reshape(bf16[2,2048,2,256]{3,2,1,0:T(2,128)(2,1)} %param.22) | data formatting | bytes 8388608 | tf_op jit(solution)/shard_map/reshape | solution.py:109
  172.1 131.1 %all-to-all-done = bf16[16,192,2048]{2,1,0:T(8,128)(2,1)} async-done(((bf16[16,192,2048]{2,1,0:T(8,128)(2,1)}), bf16[16,192,2048]{2,1,0:T(8,128)(2,1)}, u32[]{:S(2)}, u32[]{:S(2)}) %all-to-all-start) | async-done | bytes 12582944 | tf_op jit(solution)/shard_map/all_to_all | solution.py:103
  303.3 12.5 %fusion.11 = f32[8,2,192,512]{3,2,0,1:T(8,128)} fusion(bf16[2,2048,512,1]{2,1,0,3:T(8,128)(2,1)} %reshape.288, bf16[8,2,192,2048]{3,2,1,0:T(8,128)(2,1)} %bitcast.19), kind=kOutput, calls=%fused_computation.21 | convolution fusion | flops 6442450944 | bytes 23068672 | tf_op jit(solution)/shard_map/wjcd,jdf->wjcf/dot_general | solution.py:106
  315.8 9.3 %convert_bitcast_fusion = bf16[8,2,192,2048]{3,2,0,1:T(8,128)(2,1)} fusion(bf16[2,256,2048]{2,1,0:T(8,128)(2,1)S(1)} %copy-done, f32[8,2,192,512]{3,2,0,1:T(8,128)} %fusion.11), kind=kOutput, calls=%fused_computation.7 | convolution fusion | flops 3232235520 | bytes 20971520 | tf_op jit(solution)/shard_map/wjcf,jfd->wjcd/dot_general | solution.py:115
  325.0 10.7 %copy.36 = bf16[8,2,192,2048]{3,2,1,0:T(8,128)(2,1)} copy(bf16[8,2,192,2048]{3,2,0,1:T(8,128)(2,1)} %convert_bitcast_fusion) | data formatting | bytes 25165824 | tf_op jit(solution)/shard_map/convert_element_type | solution.py:117
  335.8 5.5 all-to-all-start.1
  341.5 138.8 %all-to-all-done.1 = bf16[16,192,2048]{2,1,0:T(8,128)(2,1)} async-done(((bf16[16,192,2048]{2,1,0:T(8,128)(2,1)}), bf16[16,192,2048]{2,1,0:T(8,128)(2,1)}, u32[]{:S(2)}, u32[]{:S(2)}) %all-to-all-start.1) | async-done | bytes 12582944 | tf_op jit(solution)/shard_map/all_to_all | solution.py:119
  480.3 22.5 %gather_fusion.1 = bf16[2048,2048]{1,0:T(8,128)(2,1)} fusion(bf16[3072,2048]{1,0:T(8,128)(2,1)} %bitcast.26, s32[2048]{0:T(1024)S(1)} %broadcast_clamp_fusion), kind=kCustom, calls=%fused_computation.1 | custom fusion | bytes 16785408 | tf_op jit(solution)/shard_map/gather | solution.py:126
  502.8 12.2 %fusion = bf16[256,2048]{1,0:T(8,128)(2,1)} fusion(bf16[2048,2048]{1,0:T(8,128)(2,1)} %gather_fusion.1, f32[256,8]{1,0:T(8,128)S(1)} %copy.37), kind=kLoop, calls=%fused_computation.4 | loop fusion | flops 12058624 | bytes 9445376 | tf_op jit(solution)/shard_map/reduce_sum | solution.py:127
  517.3 22.6 %reduce-scatter.2.cloned.1.call-done = bf16[256,512]{1,0:T(8,128)(2,1)} async-done(((bf16[256,2048]{1,0:T(8,128)(2,1)}), bf16[256,512]{1,0:T(8,128)(2,1)}) %reduce-scatter.2.cloned.1.call-update) | async-done | bytes 262160 | tf_op jit(solution)/shard_map/reduce_scatter | solution.py:128
  (90 shorter events, 33.9 us)
Async XLA Ops:
  7.2 308.6 %copy-start = (bf16[2,256,2048]{2,1,0:T(8,128)(2,1)S(1)}, bf16[2,256,2048]{2,1,0:T(8,128)(2,1)}, u32[]{:S(2)}) copy-start(bf16[2,256,2048]{2,1,0:T(8,128)(2,1)} %param.23) | copy-start | bytes 6291460
  7.2 39.6 %all-gather.3.cloned.1.call-start = ((), (), s32[]{:S(2)}) async-start(), calls=%async_computation.5 | async-start | bytes 1310720 | tf_op jit(solution)/shard_map/all_gather | solution.py:45
  7.9 131.8 %all-reduce.4.cloned.1.call-start = ((), (), s32[]{:S(2)}) async-start(), calls=%async_computation.3 | async-start | bytes 2097152 | tf_op jit(solution)/shard_map/psum | solution.py:85
  14.6 26.1 %copy-start.7 = (s32[1,256,8]{2,1,0:T(8,128)}, s32[1,256,8]{2,1,0:T(8,128)S(1)}, u32[]{:S(2)}) copy-start(s32[1,256,8]{2,1,0:T(8,128)S(1)} %copy.33) | copy-start | bytes 24580
  32.7 13.1 %copy-start.15 = (f32[2,512]{1,0:T(2,128)S(1)}, f32[2,512]{1,0:T(2,128)}, u32[]{:S(2)}) copy-start(f32[2,512]{1,0:T(2,128)} %param.15) | copy-start | bytes 12292
  32.7 13.6 %copy-start.13 = (bf16[2,2048]{1,0:T(2,128)(2,1)S(1)}, bf16[2,2048]{1,0:T(2,128)(2,1)}, u32[]{:S(2)}) copy-start(bf16[2,2048]{1,0:T(2,128)(2,1)} %param.13) | copy-start | bytes 24580
  45.3 8.0 %copy-start.9 = (s32[16,16,128]{2,1,0:T(8,128)}, s32[16,16,128]{2,1,0:T(8,128)S(1)}, u32[]{:S(2)}) copy-start(s32[16,16,128]{2,1,0:T(8,128)S(1)} %reduce-window.6) | copy-start | bytes 393220
  53.3 1.2 copy-start.2
  77.2 3.0 copy-start.5
  80.2 2.3 copy-start.11
  82.5 2.5 copy-start.4
  85.1 2.7 copy-start.6
  87.7 1.8 copy-start.8
  87.7 2.4 copy-start.10
  87.7 52.0 %copy-start.3 = (bf16[1,256,2048]{2,1,0:T(8,128)(2,1)S(1)}, bf16[1,256,2048]{2,1,0:T(8,128)(2,1)}, u32[]{:S(2)}) copy-start(bf16[1,256,2048]{2,1,0:T(8,128)(2,1)} %all-gather.3.cloned.1.call-done) | copy-start | bytes 3145732
  141.5 1.0 copy-start.1
  158.9 144.4 %all-to-all-start = ((bf16[16,192,2048]{2,1,0:T(8,128)(2,1)}), bf16[16,192,2048]{2,1,0:T(8,128)(2,1)}, u32[]{:S(2)}, u32[]{:S(2)}) async-start(bf16[16,192,2048]{2,1,0:T(8,128)(2,1)} %bitcast.81), calls=%async_computation | async-start | bytes 25165824 | tf_op jit(solution)/shard_map/all_to_all | solution.py:103
  335.8 5.5 %copy-start.14 = (f32[1,256,8]{1,2,0:T(8,128)S(1)}, f32[1,256,8]{1,2,0:T(8,128)}, u32[]{:S(2)}) copy-start(f32[1,256,8]{1,2,0:T(8,128)} %param.21) | copy-start | bytes 24580
  335.8 144.5 %all-to-all-start.1 = ((bf16[16,192,2048]{2,1,0:T(8,128)(2,1)}), bf16[16,192,2048]{2,1,0:T(8,128)(2,1)}, u32[]{:S(2)}, u32[]{:S(2)}) async-start(bf16[16,192,2048]{2,1,0:T(8,128)(2,1)} %bitcast.80), calls=%async_computation.1 | async-start | bytes 25165824 | tf_op jit(solution)/shard_map/all_to_all | solution.py:119
  341.3 198.7 %reduce-scatter.2.cloned.1.call-start = ((), (), s32[]{:S(2)}) async-start(), calls=%async_computation.4 | async-start | bytes 1310720 | tf_op jit(solution)/shard_map/reduce_scatter | solution.py:128
  502.8 12.3 %copy-start.12 = (bf16[256,4,128]{2,0,1:T(8,128)(2,1)S(1)}, bf16[256,4,128]{2,0,1:T(8,128)(2,1)}, u32[]{:S(2)}) copy-start(bf16[256,4,128]{2,0,1:T(8,128)(2,1)} %copy-done.11) | copy-start | bytes 786436
Sparse Core Ops, SparseCore 0:
  9.6 30.6 all-gather.2
  89.7 50.0 all-reduce.3
  515.2 24.7 reduce-scatter.1
where the time goes:
time: 550 us; the launch traced here: 548 us
  waiting for transfers between devices  335 us (61%)
  local copies, waits for them, and re-layouts  105 us (19%)
  other arithmetic  33.7 us (6%)
  matrix products  33.4 us (6%)
  between operations  16.8 us (3%)
  blocking collectives  13.6 us (2%)
  starting transfers between devices  11.2 us (2%)
    all_to_all x1, waiting for transfers between devices, per_device(): lax.all_to_all(parts.reshape(experts, capacity, full_width), 'wide', spli...  139 us
    all_to_all x1, waiting for transfers between devices, per_device(): lax.all_to_all(outgoing, 'wide', split_axis=0, concat_axis=0, tiled=True)  131 us
    psum x1, waiting for transfers between devices, per_device(): lax.psum(partial_out.astype(jnp.bfloat16), 'narrow').astype(jnp.float32)  41.4 us
    reduce_scatter x1, waiting for transfers between devices, per_device(): lax.psum_scatter(combined.astype(jnp.bfloat16), 'narrow', scatter_dimensi...  22.6 us
    gather x1, local copies, waits for them, and re-layouts, per_device(): returned.reshape(experts * capacity, full_width)[target].astype(jnp.float32)  22.5 us
    gather x1, local copies, waits for them, and re-layouts, per_device(): outgoing = padded[source_row].reshape(experts, capacity, full_width)  16 us
    unnamed x35, local copies, waits for them, and re-layouts  15.7 us
    psum x1, blocking collectives, per_device(): lax.psum((jnp.sum(queries * queries, -1), jnp.sum(keys_new * keys_new, -1...  13.6 us
  transfers between devices with their start and end apart: 5, of which 4 were waited for; matrix products, arithmetic and copies ran while one was open for 10% of the time, Pallas kernels for 0%

commit v1 on v0

--- a/solution.py
+++ b/solution.py
@@ -82,7 +82,9 @@
         .reshape(span_len, local_cols)
     )
     partial_out = jnp.dot(heads_out, w_out, preferred_element_type=jnp.float32)
-    attention = lax.psum(partial_out.astype(jnp.bfloat16), "narrow").astype(jnp.float32)
+    attention = jnp.sum(lax.all_gather(partial_out.astype(jnp.bfloat16), "narrow"), axis=0).astype(
+        jnp.float32
+    )
     after = (tokens.astype(jnp.float32) + attention).astype(jnp.bfloat16)
     after_own = lax.dynamic_slice_in_dim(after, column * share_cols, share_cols, 1)
     routed = normalize(after, norm_gain[1]).astype(jnp.bfloat16)

time: 550 us -> 576 us (1.047)
  other arithmetic: 33.7 us -> 46.7 us
  waiting for transfers between devices: 335 us -> 344 us
    all_gather x0 -> x1, waiting for transfers between devices: none -> 51.2 us  [per_device(): lax.all_gather(partial_out.astype(jnp.bfloat16), 'narrow')]
    psum x1 -> x0, waiting for transfers between devices: 41.4 us -> none  [per_device(): lax.psum(partial_out.astype(jnp.bfloat16), 'narrow').astype(jnp.float32)]
    unnamed x35 -> x25, local copies, waits for them, and re-layouts: 15.7 us -> 15 us
  transfers between devices with their start and end apart: 5 -> 5, of which waited for: 4 -> 5; matrix products, arithmetic and copies ran while one was open for 10% -> 12% of each run, Pallas kernels for 0% -> 0%
where the time goes in v1:
time: 576 us; the launch traced here: 574 us
  waiting for transfers between devices  344 us (60%)
  local copies, waits for them, and re-layouts  109 us (19%)
  other arithmetic  46.7 us (8%)
  matrix products  33.4 us (6%)
  between operations  16.7 us (3%)
  blocking collectives  13.4 us (2%)
  starting transfers between devices  11.2 us (2%)
    all_to_all x1, waiting for transfers between devices, per_device(): lax.all_to_all(parts.reshape(experts, capacity, full_width), 'wide', spli...  139 us
    all_to_all x1, waiting for transfers between devices, per_device(): lax.all_to_all(outgoing, 'wide', split_axis=0, concat_axis=0, tiled=True)  131 us
    all_gather x1, waiting for transfers between devices, per_device(): lax.all_gather(partial_out.astype(jnp.bfloat16), 'narrow')  51.2 us
    gather x1, local copies, waits for them, and re-layouts, per_device(): returned.reshape(experts * capacity, full_width)[target].astype(jnp.float32)  22.5 us
    reduce_scatter x1, waiting for transfers between devices, per_device(): lax.psum_scatter(combined.astype(jnp.bfloat16), 'narrow', scatter_dimensi...  21.8 us
    gather x1, local copies, waits for them, and re-layouts, per_device(): outgoing = padded[source_row].reshape(experts, capacity, full_width)  16 us
    unnamed x25, local copies, waits for them, and re-layouts  15 us
    psum x1, blocking collectives, per_device(): lax.psum((jnp.sum(queries * queries, -1), jnp.sum(keys_new * keys_new, -1...  13.4 us
  transfers between devices with their start and end apart: 5, of which 5 were waited for; matrix products, arithmetic and copies ran while one was open for 12% of the time, Pallas kernels for 0%

profile of v1, /device:TPU:0, one launch (start us, length us, event | category | flops | bytes accessed | tf_op | source)
XLA Modules:
  0.0 573.7 jit_solution(19708301416617871)
XLA Ops:
  13.7 8.9 %copy.24 = bf16[2048,3,512]{0,2,1:T(8,128)(2,1)} copy(bf16[2048,3,512]{2,0,1:T(8,128)(2,1)} %param.14) | data formatting | bytes 12582912 | tf_op args[2]
  22.6 4.5 fusion.74
  27.1 4.0 copy.45
  31.1 4.0 copy.31
  35.1 4.0 copy.23
  41.8 5.0 fusion.39
  48.7 13.4 %all-reduce.1 = (f32[256]{0:T(256)S(1)}, f32[256]{0:T(256)S(1)}) all-reduce(f32[256]{0:T(256)S(1)} %get-tuple-element.7, f32[256]{0:T(256)S(1)} %get-tuple-element.6), channel_id=1, replica_groups=mesh['wide'=8,'narrow'=4] {'narrow'}, use_global_device_ids=true, to_apply=%region_4.0 | all-reduce | flops 512 | bytes 4096 | tf_op jit(solution)/shard_map/psum | solution.py:54
  78.3 2.6 fusion.49
  85.0 8.1 %reduce-window.6 = s32[16,16,128]{2,1,0:T(8,128)S(1)} reduce-window(s32[16,16,128]{2,1,0:T(8,128)} %fusion.61, s32[]{:T(128)} %constant.56.clone.1), window={size=1x1x128 pad=0_0x0_0x127_0}, to_apply=%region_9.10 | reduce-window | flops 4161536 | bytes 262148 | tf_op jit(solution)/shard_map/reduce-window
  102.2 8.4 %scatter_custom_fusion = s32[3072]{0:T(1024)S(1)} fusion(s32[2048]{0:T(1024)S(1)} %bitcast.92, s32[2048]{0:T(1024)} %add_select_fusion, s32[]{:T(128)} %constant.67.clone.1), kind=kCustom, calls=%fused_computation.92 | custom fusion | bytes 12800 | tf_op jit(solution)/shard_map/scatter | solution.py:102
  110.7 51.2 %all-gather.7.cloned.1.call-done = bf16[1024,2048]{1,0:T(8,128)(2,1)} async-done(((bf16[256,2048]{1,0:T(8,128)(2,1)}), bf16[1024,2048]{1,0:T(8,128)(2,1)}) %all-gather.7.cloned.1.call-update) | async-done | bytes 4194320 | tf_op jit(solution)/shard_map/all_gather | solution.py:85
  161.9 4.3 reduce_sum.81
  169.2 16.0 %gather_fusion = bf16[3072,2048]{1,0:T(8,128)(2,1)} fusion(bf16[257,2048]{1,0:T(8,128)(2,1)S(1)} %concatenate.20, s32[3072]{0:T(1024)S(1)} %fusion.62), kind=kCustom, calls=%fused_computation | custom fusion | bytes 25178112 | tf_op jit(solution)/shard_map/gather | solution.py:104
  185.2 5.3 all-to-all-start
  190.6 7.7 %reshape.289 = bf16[2,2048,512,1]{2,1,0,3:T(8,128)(2,1)} reshape(bf16[2,2048,2,256]{3,2,1,0:T(2,128)(2,1)} %param.22) | data formatting | bytes 8388608 | tf_op jit(solution)/shard_map/reshape | solution.py:111
  198.2 131.3 %all-to-all-done = bf16[16,192,2048]{2,1,0:T(8,128)(2,1)} async-done(((bf16[16,192,2048]{2,1,0:T(8,128)(2,1)}), bf16[16,192,2048]{2,1,0:T(8,128)(2,1)}, u32[]{:S(2)}, u32[]{:S(2)}) %all-to-all-start) | async-done | bytes 12582944 | tf_op jit(solution)/shard_map/all_to_all | solution.py:105
  329.6 12.5 %fusion.11 = f32[8,2,192,512]{3,2,0,1:T(8,128)} fusion(bf16[2,2048,512,1]{2,1,0,3:T(8,128)(2,1)} %reshape.289, bf16[8,2,192,2048]{3,2,1,0:T(8,128)(2,1)} %bitcast.20), kind=kOutput, calls=%fused_computation.21 | convolution fusion | flops 6442450944 | bytes 23068672 | tf_op jit(solution)/shard_map/wjcd,jdf->wjcf/dot_general | solution.py:108
  342.1 9.3 %convert_bitcast_fusion = bf16[8,2,192,2048]{3,2,0,1:T(8,128)(2,1)} fusion(bf16[2,256,2048]{2,1,0:T(8,128)(2,1)S(1)} %copy-done, f32[8,2,192,512]{3,2,0,1:T(8,128)} %fusion.11), kind=kOutput, calls=%fused_computation.7 | convolution fusion | flops 3232235520 | bytes 20971520 | tf_op jit(solution)/shard_map/wjcf,jfd->wjcd/dot_general | solution.py:117
  351.4 10.7 %copy.36 = bf16[8,2,192,2048]{3,2,1,0:T(8,128)(2,1)} copy(bf16[8,2,192,2048]{3,2,0,1:T(8,128)(2,1)} %convert_bitcast_fusion) | data formatting | bytes 25165824 | tf_op jit(solution)/shard_map/convert_element_type | solution.py:119
  362.1 5.5 all-to-all-start.1
  368.0 138.5 %all-to-all-done.1 = bf16[16,192,2048]{2,1,0:T(8,128)(2,1)} async-done(((bf16[16,192,2048]{2,1,0:T(8,128)(2,1)}), bf16[16,192,2048]{2,1,0:T(8,128)(2,1)}, u32[]{:S(2)}, u32[]{:S(2)}) %all-to-all-start.1) | async-done | bytes 12582944 | tf_op jit(solution)/shard_map/all_to_all | solution.py:121
  506.6 22.5 %gather_fusion.1 = bf16[2048,2048]{1,0:T(8,128)(2,1)} fusion(bf16[3072,2048]{1,0:T(8,128)(2,1)} %bitcast.27, s32[2048]{0:T(1024)S(1)} %broadcast_clamp_fusion), kind=kCustom, calls=%fused_computation.1 | custom fusion | bytes 16785408 | tf_op jit(solution)/shard_map/gather | solution.py:128
  529.1 12.2 %fusion = bf16[256,2048]{1,0:T(8,128)(2,1)} fusion(bf16[2048,2048]{1,0:T(8,128)(2,1)} %gather_fusion.1, f32[256,8]{1,0:T(8,128)S(1)} %copy.37), kind=kLoop, calls=%fused_computation.4 | loop fusion | flops 12058624 | bytes 9445376 | tf_op jit(solution)/shard_map/reduce_sum | solution.py:129
  543.6 21.8 %reduce-scatter.2.cloned.1.call-done = bf16[256,512]{1,0:T(8,128)(2,1)} async-done(((bf16[256,2048]{1,0:T(8,128)(2,1)}), bf16[256,512]{1,0:T(8,128)(2,1)}) %reduce-scatter.2.cloned.1.call-update) | async-done | bytes 262160 | tf_op jit(solution)/shard_map/reduce_scatter | solution.py:130
  (81 shorter events, 45.3 us)
Async XLA Ops:
  7.2 334.9 %copy-start = (bf16[2,256,2048]{2,1,0:T(8,128)(2,1)S(1)}, bf16[2,256,2048]{2,1,0:T(8,128)(2,1)}, u32[]{:S(2)}) copy-start(bf16[2,256,2048]{2,1,0:T(8,128)(2,1)} %param.23) | copy-start | bytes 6291460
  7.2 33.1 %all-gather.5.cloned.1.call-start = ((), (), s32[]{:S(2)}) async-start(), calls=%async_computation.4 | async-start | bytes 1310720 | tf_op jit(solution)/shard_map/all_gather | solution.py:45
  7.9 153.9 %all-gather.7.cloned.1.call-start = ((), (), s32[]{:S(2)}) async-start(), calls=%async_computation.5 | async-start | bytes 5242880 | tf_op jit(solution)/shard_map/all_gather | solution.py:85
  31.1 8.0 %copy-start.10 = (f32[2,512]{1,0:T(2,128)S(1)}, f32[2,512]{1,0:T(2,128)}, u32[]{:S(2)}) copy-start(f32[2,512]{1,0:T(2,128)} %param.15) | copy-start | bytes 12292
  31.1 8.5 %copy-start.8 = (bf16[2,2048]{1,0:T(2,128)(2,1)S(1)}, bf16[2,2048]{1,0:T(2,128)(2,1)}, u32[]{:S(2)}) copy-start(bf16[2,2048]{1,0:T(2,128)(2,1)} %param.13) | copy-start | bytes 24580
  46.7 1.2 copy-start.2
  70.5 3.0 copy-start.5
  75.8 2.5 copy-start.4
  78.3 2.6 copy-start.6
  81.0 1.8 copy-start.7
  82.7 83.4 %copy-start.3 = (bf16[1,256,2048]{2,1,0:T(8,128)(2,1)S(1)}, bf16[1,256,2048]{2,1,0:T(8,128)(2,1)}, u32[]{:S(2)}) copy-start(bf16[1,256,2048]{2,1,0:T(8,128)(2,1)} %all-gather.5.cloned.1.call-done) | copy-start | bytes 3145732
  167.8 1.0 copy-start.1
  185.2 144.4 %all-to-all-start = ((bf16[16,192,2048]{2,1,0:T(8,128)(2,1)}), bf16[16,192,2048]{2,1,0:T(8,128)(2,1)}, u32[]{:S(2)}, u32[]{:S(2)}) async-start(bf16[16,192,2048]{2,1,0:T(8,128)(2,1)} %bitcast.82), calls=%async_computation | async-start | bytes 25165824 | tf_op jit(solution)/shard_map/all_to_all | solution.py:105
  362.1 5.8 %copy-start.9 = (f32[1,256,8]{1,2,0:T(8,128)S(1)}, f32[1,256,8]{1,2,0:T(8,128)}, u32[]{:S(2)}) copy-start(f32[1,256,8]{1,2,0:T(8,128)} %param.21) | copy-start | bytes 24580
  362.1 144.5 %all-to-all-start.1 = ((bf16[16,192,2048]{2,1,0:T(8,128)(2,1)}), bf16[16,192,2048]{2,1,0:T(8,128)(2,1)}, u32[]{:S(2)}, u32[]{:S(2)}) async-start(bf16[16,192,2048]{2,1,0:T(8,128)(2,1)} %bitcast.81), calls=%async_computation.1 | async-start | bytes 25165824 | tf_op jit(solution)/shard_map/all_to_all | solution.py:121
  367.5 197.8 %reduce-scatter.2.cloned.1.call-start = ((), (), s32[]{:S(2)}) async-start(), calls=%async_computation.3 | async-start | bytes 1310720 | tf_op jit(solution)/shard_map/reduce_scatter | solution.py:130
Sparse Core Ops, SparseCore 0:
  9.6 30.6 all-gather.4
  82.8 78.9 all-gather.6
  541.5 23.8 reduce-scatter.1
